TPU v7x, 32 devices: a whole 2x2x4 slice. The times are simulated.
32 devices in a mesh: shard: 4 (over y, x), ctx: 2 (over core), tp: 4 (over z).
Axes of the slice: x: 2, y: 2, z: 4, core: 2. Of those that a mesh axis runs over, the one named last changes fastest.
Arguments:
- tokens: bfloat16 [4, 1024, 1536], P('shard', ('ctx', 'tp')), may hold values from -6 to 6
- cotangent: bfloat16 [4, 1024, 1536], P('shard', ('ctx', 'tp')), may hold values from -6 to 6
- lengths: int32 [4], P('shard'), may hold values from 256 to 1024, as said below
- w_qkv: bfloat16 [1536, 3, 1536], P(('shard', 'ctx'), None, 'tp'), may hold values from -0.15625 to 0.15625
- w_forget: bfloat16 [1536, 24], P(('shard', 'ctx'), 'tp'), may hold values from -0.15625 to 0.15625
- forget_bias: float32 [24], replicated, may hold values from 3 to 8
- w_ogate: bfloat16 [1536, 1536], P(('shard', 'ctx'), 'tp'), may hold values from -0.15625 to 0.15625
- w_out: bfloat16 [1536, 1536], P(('shard', 'ctx'), 'tp'), may hold values from -0.625 to 0.625
- w_gu: bfloat16 [1536, 2, 4096], P(('shard', 'ctx'), None, 'tp'), may hold values from -0.15625 to 0.15625
- w_down: bfloat16 [1536, 4096], P(('shard', 'ctx'), 'tp'), may hold values from -0.09375 to 0.09375
- gain_attn: float32 [1536], replicated, may hold values from 0.5 to 1.5
- gain_mlp: float32 [1536], replicated, may hold values from 0.5 to 1.5
- qk_gain: float32 [2, 64], replicated, may hold values from 1 to 2
Outputs:
- output: bfloat16 [4, 1024, 1536], P('shard', ('ctx', 'tp'))
- input_grad: bfloat16 [4, 1024, 1536], P('shard', ('ctx', 'tp'))
- grad_qkv: float32 [1536, 3, 1536], P(('shard', 'ctx'), None, 'tp')
- grad_forget: float32 [1536, 24], P(('shard', 'ctx'), 'tp')
- grad_forget_bias: float32 [24], replicated
- grad_ogate: float32 [1536, 1536], P(('shard', 'ctx'), 'tp')
- grad_out: float32 [1536, 1536], P(('shard', 'ctx'), 'tp')
- grad_gu: float32 [1536, 2, 4096], P(('shard', 'ctx'), None, 'tp')
- grad_down: float32 [1536, 4096], P(('shard', 'ctx'), 'tp')
- grad_gain_attn: float32 [1536], replicated
- grad_gain_mlp: float32 [1536], replicated
- grad_qk_gain: float32 [2, 64], replicated
Inputs may be any that keep to these rules, and one draw needn't show every extreme that they name: `lengths`: real tokens of a slot; positions at or past it are padding; both the least and the most value occur in every draw.
All inputs are finite; a program needn't handle non-finite values.
Results may differ from a plain program's by a relative error of at most 0.04.
Values may be sent and summed in bfloat16 or wider, within the bound.
No kernel may reach another device: no remote copies, remote signals or barrier semaphores. Data moves between devices by JAX's collectives and lax.ppermute only.
A program may use at most 128 MiB of HBM per device.

v0:
```python
import math
import jax
import jax.numpy as jnp
from jax import lax
from jax.sharding import PartitionSpec as P

epsilon = 1e-06


def shifted(block, axis, distance):
    devices = range(lax.axis_size(axis))
    route = [(i - distance, i) for i in devices if i - distance in devices]
    return lax.ppermute(block, axis, route)


def norm_rows(values, gain):
    return values * lax.rsqrt(jnp.mean(values * values, axis=-1, keepdims=True) + epsilon) * gain


def product(left, right):
    return jnp.dot(left, right, preferred_element_type=jnp.float32)


def product_t(left, right):
    return lax.dot_general(
        left, right, (((1,), (1,)), ((), ())), preferred_element_type=jnp.float32
    )


def outer_rows(left, right):
    return lax.dot_general(
        left, right, (((0,), (0,)), ((), ())), preferred_element_type=jnp.float32
    )


def body(
    tokens,
    cotangent,
    lengths,
    w_qkv,
    w_forget,
    forget_bias,
    w_ogate,
    w_out,
    w_gu,
    w_down,
    gain_attn,
    gain_mlp,
    qk_gain,
):
    slot_count, own_rows, model_width = tokens.shape
    tensor_size = lax.axis_size("tp")
    tensor_place = lax.axis_index("tp")
    span_index = lax.axis_index("ctx")
    half_rows = own_rows * tensor_size
    row_count = slot_count * half_rows
    local_heads = w_forget.shape[1]
    head_size = qk_gain.shape[1]
    head_cols = local_heads * head_size
    hidden_units = w_down.shape[1]
    item_count = slot_count * local_heads
    score_scale = 1.0 / math.sqrt(head_size)
    own_start = tensor_place * own_rows
    full_tokens, full_cot = (
        lax.all_gather(tokens, "tp", axis=1, tiled=True),
        lax.all_gather(cotangent, "tp", axis=1, tiled=True),
    )
    qkv_full, forget_full, ogate_full, out_full, gu_full, down_full = (
        lax.all_gather(w_qkv, ("shard", "ctx"), axis=0, tiled=True),
        lax.all_gather(w_forget, ("shard", "ctx"), axis=0, tiled=True),
        lax.all_gather(w_ogate, ("shard", "ctx"), axis=0, tiled=True),
        lax.all_gather(w_out, ("shard", "ctx"), axis=0, tiled=True),
        lax.all_gather(w_gu, ("shard", "ctx"), axis=0, tiled=True),
        lax.all_gather(w_down, ("shard", "ctx"), axis=0, tiled=True),
    )
    qkv_flat = qkv_full.reshape(model_width, 3 * head_cols)
    gu_flat = gu_full.reshape(model_width, 2 * hidden_units)

    def own_slice(values):
        return lax.dynamic_slice_in_dim(
            values.reshape(slot_count, half_rows, values.shape[-1]), own_start, own_rows, 1
        )

    positions = span_index * half_rows + jnp.arange(half_rows, dtype=jnp.int32)
    valid_rows = (positions[None, :] < lengths[:, None]).astype(jnp.float32).reshape(row_count, 1)
    own_positions = span_index * half_rows + own_start + jnp.arange(own_rows, dtype=jnp.int32)
    valid_own = (own_positions[None, :] < lengths[:, None]).astype(jnp.float32)[:, :, None]
    residual = full_tokens.reshape(row_count, model_width).astype(jnp.float32)
    normed = norm_rows(residual, gain_attn).astype(jnp.bfloat16)
    qkv_rows = product(normed, qkv_flat).reshape(row_count, 3, head_cols)
    query_raw = qkv_rows[:, 0].reshape(row_count, local_heads, head_size)
    key_raw = qkv_rows[:, 1].reshape(row_count, local_heads, head_size)
    queries = (
        norm_rows(query_raw, qk_gain[0])
        .astype(jnp.bfloat16)
        .reshape(slot_count, half_rows, head_cols)
    )
    keys_here = (
        norm_rows(key_raw, qk_gain[1])
        .astype(jnp.bfloat16)
        .reshape(slot_count, half_rows, head_cols)
    )
    values_here = qkv_rows[:, 2].astype(jnp.bfloat16).reshape(slot_count, half_rows, head_cols)
    bias_here = lax.dynamic_slice_in_dim(forget_bias, tensor_place * local_heads, local_heads)
    forget_pre = (product(normed, forget_full) + bias_here).reshape(
        slot_count, half_rows, local_heads
    )
    cum_here = jnp.cumsum(jax.nn.log_sigmoid(forget_pre), axis=1)
    keys_left, values_left = shifted((keys_here, values_here), "ctx", 1)
    cum_left = shifted(cum_here, "ctx", 1)
    cum_query = cum_here + cum_left[:, -1:, :]

    def by_head(values):
        shaped = values.reshape(slot_count, half_rows, local_heads, head_size)
        return jnp.transpose(shaped, (0, 2, 1, 3)).reshape(item_count, half_rows, head_size)

    def by_head_cum(values):
        return jnp.transpose(values, (0, 2, 1)).reshape(item_count, half_rows)

    def to_slots(values):
        shaped = values.reshape(slot_count, local_heads, half_rows, head_size)
        return jnp.transpose(shaped, (0, 2, 1, 3)).reshape(slot_count, half_rows, head_cols)

    def to_slots_cum(values):
        return jnp.transpose(values.reshape(slot_count, local_heads, half_rows), (0, 2, 1))

    q_items = by_head(queries)
    k_items = jnp.concatenate([by_head(keys_left), by_head(keys_here)], axis=1)
    v_items = jnp.concatenate([by_head(values_left), by_head(values_here)], axis=1)
    cq_items = by_head_cum(cum_query)
    ck_items = jnp.concatenate([by_head_cum(cum_left), cq_items], axis=1)
    place_ids = jnp.arange(half_rows, dtype=jnp.int32)
    earlier = jnp.broadcast_to(span_index > 0, (half_rows, half_rows))
    allowed = jnp.concatenate([earlier, place_ids[None, :] <= place_ids[:, None]], axis=1)

    def score_block(query_block, key_block, cum_rows, cum_cols):
        score_raw = (
            product_t(query_block, key_block) * score_scale + cum_rows[:, None] - cum_cols[None, :]
        )
        return jnp.where(allowed, score_raw, -jnp.inf)

    def forward_item(pieces):
        query_block, key_block, value_block, cum_rows, cum_cols = pieces
        score_vals = score_block(query_block, key_block, cum_rows, cum_cols)
        row_max = jnp.max(score_vals, axis=1, keepdims=True)
        expo = jnp.exp(score_vals - row_max)
        row_total = jnp.sum(expo, axis=1, keepdims=True)
        attn_probs = (expo / row_total).astype(jnp.bfloat16)
        return (product(attn_probs, value_block), (row_max + jnp.log(row_total))[:, 0])

    attended_items, lse_items = lax.map(
        forward_item, (q_items, k_items, v_items, cq_items, ck_items)
    )
    attended_rows = to_slots(attended_items).reshape(row_count, head_cols)
    opener = jax.nn.sigmoid(product(normed, ogate_full))
    gated = (attended_rows * opener).astype(jnp.bfloat16)
    branch_part = product_t(gated, out_full)
    branch_full = lax.psum(branch_part, "tp")
    middle = residual + branch_full
    middle_share = own_slice(middle)
    normed_mid = norm_rows(middle, gain_mlp).astype(jnp.bfloat16)
    both = product(normed_mid, gu_flat).reshape(row_count, 2, hidden_units)
    gate_pre = both[:, 0]
    up_pre = both[:, 1]
    gate_sig = jax.nn.sigmoid(gate_pre)
    hidden = (gate_pre * gate_sig * up_pre).astype(jnp.bfloat16)
    down_share = lax.psum_scatter(
        product_t(hidden, down_full)
        .reshape(slot_count, half_rows, model_width)
        .astype(jnp.bfloat16),
        "tp",
        scatter_dimension=1,
        tiled=True,
    ).astype(jnp.float32)
    output = (valid_own * (middle_share + down_share)).astype(jnp.bfloat16)
    cot_rows = full_cot.reshape(row_count, model_width) * valid_rows.astype(jnp.bfloat16)
    d_hidden = product(cot_rows, down_full)
    d_gate = d_hidden * up_pre * gate_sig * (1.0 + gate_pre * (1.0 - gate_sig))
    d_up = d_hidden * gate_pre * gate_sig
    d_both = (
        jnp.stack([d_gate, d_up], axis=1).astype(jnp.bfloat16).reshape(row_count, 2 * hidden_units)
    )
    grad_down = outer_rows(cot_rows, hidden)
    grad_gu = outer_rows(normed_mid, d_both).reshape(model_width, 2, hidden_units)
    d_mid_terms = product_t(d_both, gu_flat)
    d_normed_mid = lax.psum(d_mid_terms, "tp")
    _, pull_mid = jax.vjp(norm_rows, middle, gain_mlp)
    d_middle_norm, d_gain_mlp_all = pull_mid(d_normed_mid)
    d_middle = d_middle_norm + cot_rows.astype(jnp.float32)
    feat_share = model_width // tensor_size
    owner = jnp.arange(model_width, dtype=jnp.int32) // feat_share == tensor_place
    d_gain_mlp_own = jnp.where(owner, d_gain_mlp_all, 0.0)
    d_branch = d_middle.astype(jnp.bfloat16)
    d_middle_share = own_slice(d_middle)
    d_gated = product(d_branch, out_full)
    grad_out = outer_rows(d_branch, gated)
    d_attended = (d_gated * opener).astype(jnp.bfloat16)
    d_open = (d_gated * attended_rows * opener * (1.0 - opener)).astype(jnp.bfloat16)
    grad_ogate = outer_rows(normed, d_open)
    da_items = by_head(d_attended.reshape(slot_count, half_rows, head_cols))

    def backward_item(pieces):
        query_block, key_block, value_block, cum_rows, cum_cols, lse_block, grad_block = pieces
        score_vals = score_block(query_block, key_block, cum_rows, cum_cols)
        attn_probs = jnp.exp(score_vals - lse_block[:, None])
        d_probs = product_t(grad_block, value_block)
        centre = jnp.sum(attn_probs * d_probs, axis=1, keepdims=True)
        d_scores = (attn_probs * (d_probs - centre)).astype(jnp.bfloat16)
        d_query_block = product(d_scores, key_block) * score_scale
        d_key_block = outer_rows(d_scores, query_block) * score_scale
        d_value_block = outer_rows(attn_probs.astype(jnp.bfloat16), grad_block)
        d_cum_rows = jnp.sum(d_scores, axis=1, dtype=jnp.float32)
        d_cum_cols = -jnp.sum(d_scores, axis=0, dtype=jnp.float32)
        return (d_query_block, d_key_block, d_value_block, d_cum_rows, d_cum_cols)

    dq_items, dk_items, dv_items, dcq_items, dck_items = lax.map(
        backward_item, (q_items, k_items, v_items, cq_items, ck_items, lse_items, da_items)
    )
    dc_own = dcq_items + dck_items[:, half_rows:]
    dc_left = dck_items[:, :half_rows]
    dc_left = dc_left.at[:, -1].add(jnp.sum(dc_own, axis=1))
    back_keys, back_values, back_cum = (
        shifted(to_slots(dk_items[:, :half_rows]).astype(jnp.bfloat16), "ctx", -1).astype(
            jnp.float32
        ),
        shifted(to_slots(dv_items[:, :half_rows]).astype(jnp.bfloat16), "ctx", -1).astype(
            jnp.float32
        ),
        shifted(to_slots_cum(dc_left).astype(jnp.bfloat16), "ctx", -1).astype(jnp.float32),
    )
    d_query = to_slots(dq_items).reshape(row_count, local_heads, head_size)
    d_key = (to_slots(dk_items[:, half_rows:]) + back_keys).reshape(
        row_count, local_heads, head_size
    )
    d_value = (to_slots(dv_items[:, half_rows:]) + back_values).reshape(row_count, head_cols)
    d_cum = to_slots_cum(dc_own) + back_cum
    d_log = jnp.flip(jnp.cumsum(jnp.flip(d_cum, 1), axis=1), 1)
    d_forget = d_log * jax.nn.sigmoid(-forget_pre)
    d_bias_own = jnp.sum(d_forget, axis=(0, 1))
    d_forget_low = d_forget.reshape(row_count, local_heads).astype(jnp.bfloat16)
    grad_forget = outer_rows(normed, d_forget_low)
    _, pull_query = jax.vjp(norm_rows, query_raw, qk_gain[0])
    d_query_raw, d_query_gain = pull_query(d_query)
    _, pull_key = jax.vjp(norm_rows, key_raw, qk_gain[1])
    d_key_raw, d_key_gain = pull_key(d_key)
    d_mixed = (
        jnp.stack(
            [
                d_query_raw.reshape(row_count, head_cols),
                d_key_raw.reshape(row_count, head_cols),
                d_value,
            ],
            axis=1,
        )
        .astype(jnp.bfloat16)
        .reshape(row_count, 3 * head_cols)
    )
    grad_qkv = outer_rows(normed, d_mixed).reshape(model_width, 3, head_cols)
    d_normed = (
        product_t(d_mixed, qkv_flat)
        + product_t(d_open, ogate_full)
        + product_t(d_forget_low, forget_full)
    )
    root = lax.rsqrt(jnp.mean(residual * residual, axis=1, keepdims=True) + epsilon)
    unit = residual * root
    d_unit = d_normed * gain_attn
    dot_part = (jnp.sum(d_unit * unit, axis=1) / model_width).reshape(slot_count, half_rows)
    d_unit_share, dot_full = (
        lax.psum_scatter(
            d_unit.reshape(slot_count, half_rows, model_width).astype(jnp.bfloat16),
            "tp",
            scatter_dimension=1,
            tiled=True,
        ).astype(jnp.float32),
        lax.psum_scatter(
            dot_part.astype(jnp.bfloat16), "tp", scatter_dimension=1, tiled=True
        ).astype(jnp.float32),
    )
    unit_share = own_slice(unit)
    root_share = own_slice(root)
    input_grad = (
        d_middle_share + root_share * (d_unit_share - unit_share * dot_full[:, :, None])
    ).astype(jnp.bfloat16)
    grad_parts = (
        lax.psum_scatter(
            grad_qkv.astype(jnp.bfloat16), ("shard", "ctx"), scatter_dimension=0, tiled=True
        ).astype(jnp.float32),
        lax.psum_scatter(
            grad_forget.astype(jnp.bfloat16), ("shard", "ctx"), scatter_dimension=0, tiled=True
        ).astype(jnp.float32),
        lax.psum_scatter(
            grad_ogate.astype(jnp.bfloat16), ("shard", "ctx"), scatter_dimension=0, tiled=True
        ).astype(jnp.float32),
        lax.psum_scatter(
            grad_out.astype(jnp.bfloat16), ("shard", "ctx"), scatter_dimension=0, tiled=True
        ).astype(jnp.float32),
        lax.psum_scatter(
            grad_gu.astype(jnp.bfloat16), ("shard", "ctx"), scatter_dimension=0, tiled=True
        ).astype(jnp.float32),
        lax.psum_scatter(
            grad_down.astype(jnp.bfloat16), ("shard", "ctx"), scatter_dimension=0, tiled=True
        ).astype(jnp.float32),
    )
    bias_full = lax.dynamic_update_slice_in_dim(
        jnp.zeros(forget_bias.shape, jnp.float32), d_bias_own, tensor_place * local_heads, 0
    )
    gain_attn_part = jnp.sum(d_normed * unit, axis=0)
    small_parts = lax.psum(
        (gain_attn_part, d_gain_mlp_own, jnp.stack([d_query_gain, d_key_gain]), bias_full),
        ("shard", "ctx", "tp"),
    )
    return (
        output,
        input_grad,
        grad_parts[0],
        grad_parts[1],
        small_parts[3],
        grad_parts[2],
        grad_parts[3],
        grad_parts[4],
        grad_parts[5],
        small_parts[0],
        small_parts[1],
        small_parts[2],
    )


def solution(mesh):
    return jax.shard_map(
        body,
        mesh=mesh,
        in_specs=(
            P("shard", ("ctx", "tp"), None),
            P("shard", ("ctx", "tp"), None),
            P("shard"),
            P(("shard", "ctx"), None, "tp"),
            P(("shard", "ctx"), "tp"),
            P(),
            P(("shard", "ctx"), "tp"),
            P(("shard", "ctx"), "tp"),
            P(("shard", "ctx"), None, "tp"),
            P(("shard", "ctx"), "tp"),
            P(),
            P(),
            P(),
        ),
        out_specs=(
            P("shard", ("ctx", "tp"), None),
            P("shard", ("ctx", "tp"), None),
            P(("shard", "ctx"), None, "tp"),
            P(("shard", "ctx"), "tp"),
            P(),
            P(("shard", "ctx"), "tp"),
            P(("shard", "ctx"), "tp"),
            P(("shard", "ctx"), None, "tp"),
            P(("shard", "ctx"), "tp"),
            P(),
            P(),
            P(),
        ),
        check_vma=False,
    )
```

profile of v0, /device:TPU:0, one launch (start us, length us, event | category | flops | bytes accessed | tf_op | source)
XLA Modules:
  0.0 1049.7 jit_solution(11627350117377922482)
XLA Ops:
  11.9 10.6 %all-gather = bf16[8,192,6]{1,2,0:T(8,128)(2,1)S(1)} all-gather(bf16[1,192,6]{1,2,0:T(8,128)(2,1)} %bitcast.510), channel_id=1, replica_groups=mesh['shard'=4,'ctx'=2,'tp'=4] {'shard','ctx'}, dimensions={0}, use_global_device_ids=true | all-gather | bytes 20736 | tf_op jit(solution)/shard_map/all_gather | solution.py:70
  24.6 24.8 %all-gather.9.cloned.1.call-done = bf16[1,512,1536]{2,1,0:T(8,128)(2,1)} async-done(((bf16[1,128,1536]{2,1,0:T(8,128)(2,1)}), bf16[1,512,1536]{2,1,0:T(8,128)(2,1)}) %all-gather.9.cloned.1.call-update) | async-done | bytes 1572880 | tf_op jit(solution)/shard_map/all_gather | solution.py:65
  59.5 24.7 %all-gather.11.cloned.1.call-done = bf16[1536,3,384]{2,0,1:T(8,128)(2,1)} async-done(((bf16[192,3,384]{2,0,1:T(8,128)(2,1)}), bf16[1536,3,384]{2,0,1:T(8,128)(2,1)}) %all-gather.11.cloned.1.call-update) | async-done | bytes 3538960 | tf_op jit(solution)/shard_map/all_gather | solution.py:69
  84.2 6.1 copy.92
  90.3 4.1 fusion.41
  96.7 2.9 collective-permute-start
  106.8 3.3 fusion.74
  110.1 2.2 copy.94
  112.2 2.2 copy.101
  118.7 37.0 %while.31 = (s32[]{:T(128)}, f32[6,512,64]{1,2,0:T(8,128)}, f32[6,512]{1,0:T(8,128)S(1)}, bf16[6,512,64]{2,1,0:T(8,128)(2,1)}, bf16[6,1024,64]{2,1,0:T(8,128)(2,...) while((s32[]{:T(128)}, f32[6,512,64]{1,2,0:T(8,128)}, ...), condition=%wide.region_8.9_spmd, body=%wide.region_5.8_spmd.sunk | while | flops 139460096 | bytes 7643265 | solution.py:151
  122.5 2.2 fusion.162
  128.7 2.3 fusion.162
  134.9 2.2 fusion.162
  141.0 2.2 fusion.162
  147.2 2.2 fusion.162
  153.3 2.2 fusion.162
  156.2 3.4 fusion.84
  159.7 4.0 fusion.126
  168.9 116.0 %all-reduce.5.cloned.1.call-done = f32[512,1536]{1,0:T(8,128)} async-done(((f32[512,1536]{1,0:T(8,128)}), f32[512,1536]{1,0:T(8,128)}) %all-reduce.5.cloned.1.call-update) | async-done | bytes 3145744 | tf_op jit(solution)/shard_map/psum | solution.py:158
  284.9 2.8 multiply_reduce_fusion.5
  289.3 42.5 %all-gather.17.cloned.1.call-done = bf16[1536,2,1024]{2,0,1:T(8,128)(2,1)} async-done(((bf16[192,2,1024]{2,0,1:T(8,128)(2,1)}), bf16[1536,2,1024]{2,0,1:T(8,128)(2,1)}) %all-gather.17.cloned.1.call-update) | async-done | bytes 6291472 | tf_op jit(solution)/shard_map/all_gather | solution.py:73
  331.8 8.7 copy.104
  340.5 8.1 fusion.36
  348.6 21.9 %all-gather.21.cloned.1.call-done = bf16[1,512,1536]{2,1,0:T(8,128)(2,1)} async-done(((bf16[1,128,1536]{2,1,0:T(8,128)(2,1)}), bf16[1,512,1536]{2,1,0:T(8,128)(2,1)}) %all-gather.21.cloned.1.call-update) | async-done | bytes 1572880 | tf_op jit(solution)/shard_map/all_gather | solution.py:66
  370.5 33.1 %all-gather.19.cloned.1.call-done = bf16[1536,1024]{1,0:T(8,128)(2,1)} async-done(((bf16[192,1024]{1,0:T(8,128)(2,1)}), bf16[1536,1024]{1,0:T(8,128)(2,1)}) %all-gather.19.cloned.1.call-update) | async-done | bytes 3145744 | tf_op jit(solution)/shard_map/all_gather | solution.py:74
  403.6 5.9 fusion.52
  410.9 8.0 convolution_bitcast_fusion.2
  423.5 6.7 fusion.47
  430.5 109.7 %all-reduce.7.cloned.1.call-done = f32[512,1536]{1,0:T(8,128)} async-done(((f32[512,1536]{1,0:T(8,128)}), f32[512,1536]{1,0:T(8,128)}) %all-reduce.7.cloned.1.call-update) | async-done | bytes 3145744 | tf_op jit(solution)/shard_map/psum | solution.py:186
  540.2 3.4 multiply_reduce_fusion.1
  543.7 3.0 fusion.46
  548.5 2.2 copy.105
  552.2 97.2 %while.32 = (s32[]{:T(128)}, f32[6,512,64]{1,2,0:T(8,128)}, f32[6,1024,64]{1,2,0:T(8,128)}, f32[6,1024,64]{1,2,0:T(8,128)}, f32[6,512]{1,0:T(8,128)}, /*index=5*...) while((s32[]{:T(128)}, f32[6,512,64]{1,2,0:T(8,128)}, ...), condition=%wide.region_18.19_spmd, body=%wide.region_14.18_spmd.sunk | while | flops 342981632 | bytes 20376776 | solution.py:216
  555.3 2.1 multiply_reduce_fusion.11
  571.5 2.1 multiply_reduce_fusion.11
  587.6 2.1 multiply_reduce_fusion.11
  603.8 2.1 multiply_reduce_fusion.11
  620.1 2.1 multiply_reduce_fusion.11
  636.2 2.1 multiply_reduce_fusion.11
  651.3 2.1 slice.88
  667.2 2.3 fusion.80
  672.4 2.7 rev.7
  676.4 4.1 reduce-window.16
  691.2 2.7 rev.8
  695.9 2.6 convolution_convert_fusion.6
  700.6 2.3 multiply_reduce_fusion.6
  707.6 2.3 convolution_bitcast_fusion.3
  711.4 3.4 multiply_reduce_fusion.2
  715.7 6.4 convolution_convert_fusion.2
  722.2 3.7 convolution_convert_fusion.5
  729.0 5.8 convolution_convert_fusion.1
  734.9 3.1 maximum_convert_fusion
  738.0 4.0 copy.114
  742.0 8.9 convolution_convert_fusion
  751.6 2.1 fusion.89
  755.5 41.1 %all-reduce.1 = (f32[24]{0:T(128)}, f32[1536]{0:T(1024)}, f32[1536]{0:T(1024)}, f32[2,64]{1,0:T(2,128)}) all-reduce(f32[24]{0:T(128)S(1)} %dynamic_update_slice.28, f32[1536]{0:T(1024)S(1)} %get-tuple-element.207, f32[1536]{0:T(1024)S(1)} %fusion.108, ...), channel_id=1, replica_groups=mesh['shard'=4,'ctx'=2,'tp'=4] {'shard','ctx','tp'}, use_global_device_ids=true, to_apply=%region_30.31 | all-reduce | flops 3224 | bytes 25792 | tf_op jit(solution)/shard_map/psum | solution.py:308
  797.5 8.2 reduce-scatter.26.cloned.1.call-done
  807.7 37.9 %reduce-scatter.20.cloned.1.call-done = bf16[192,384]{1,0:T(8,128)(2,1)} async-done(((bf16[1536,384]{1,0:T(8,128)(2,1)}), bf16[192,384]{1,0:T(8,128)(2,1)}) %reduce-scatter.20.cloned.1.call-update) | async-done | bytes 147472 | tf_op jit(solution)/shard_map/reduce_scatter | solution.py:291
  847.2 38.6 %reduce-scatter.22.cloned.1.call-done = bf16[192,384]{1,0:T(8,128)(2,1)} async-done(((bf16[1536,384]{1,0:T(8,128)(2,1)}), bf16[192,384]{1,0:T(8,128)(2,1)}) %reduce-scatter.22.cloned.1.call-update) | async-done | bytes 147472 | tf_op jit(solution)/shard_map/reduce_scatter | solution.py:294
  887.5 36.4 %reduce-scatter.16.cloned.1.call-done = bf16[1,128,1536]{2,1,0:T(8,128)(2,1)} async-done(((bf16[1,512,1536]{2,1,0:T(8,128)(2,1)}), bf16[1,128,1536]{2,1,0:T(8,128)(2,1)}) %reduce-scatter.16.cloned.1.call-update) | async-done | bytes 393232 | tf_op jit(solution)/shard_map/reduce_scatter | solution.py:269
  923.9 2.2 fusion.83
  926.1 48.2 %reduce-scatter.18.cloned.1.call-done = bf16[192,3,384]{2,0,1:T(8,128)(2,1)} async-done(((bf16[1536,3,384]{2,0,1:T(8,128)(2,1)}), bf16[192,3,384]{2,0,1:T(8,128)(2,1)}) %reduce-scatter.18.cloned.1.call-update) | async-done | bytes 442384 | tf_op jit(solution)/shard_map/reduce_scatter | solution.py:285
  976.3 63.0 %reduce-scatter.24.cloned.1.call-done = bf16[192,2,1024]{2,0,1:T(8,128)(2,1)} async-done(((bf16[1536,2,1024]{2,0,1:T(8,128)(2,1)}), bf16[192,2,1024]{2,0,1:T(8,128)(2,1)}) %reduce-scatter.24.cloned.1.call-update) | async-done | bytes 786448 | tf_op jit(solution)/shard_map/reduce_scatter | solution.py:297
  1039.3 3.1 copy.116
  (403 shorter events, 209.6 us)
Async XLA Ops:
  7.2 17.4 %copy-start.69 = (f32[24]{0:T(128)S(1)}, f32[24]{0:T(128)}, u32[]{:S(2)}) copy-start(f32[24]{0:T(128)} %param.24) | copy-start | bytes 292
  7.2 42.2 %all-gather.9.cloned.1.call-start = ((), (), s32[]{:S(2)}) async-start(), calls=%async_computation.9 | async-start | bytes 1966080 | tf_op jit(solution)/shard_map/all_gather | solution.py:65
  7.9 76.3 %all-gather.11.cloned.1.call-start = ((), (), s32[]{:S(2)}) async-start(), calls=%async_computation.10 | async-start | bytes 3981312 | tf_op jit(solution)/shard_map/all_gather | solution.py:69
  8.7 42.5 %copy-start.59 = (f32[1536]{0:T(1024)S(1)}, f32[1536]{0:T(1024)}, u32[]{:S(2)}) copy-start(f32[1536]{0:T(1024)} %param.29) | copy-start | bytes 18436
  8.7 147.0 %all-gather.13.cloned.1.call-start = ((), (), s32[]{:S(2)}) async-start(), calls=%async_computation.11 | async-start | bytes 1327104 | tf_op jit(solution)/shard_map/all_gather | solution.py:71
  9.4 150.3 %all-gather.15.cloned.1.call-start = ((), (), s32[]{:S(2)}) async-start(), calls=%async_computation.12 | async-start | bytes 1327104 | tf_op jit(solution)/shard_map/all_gather | solution.py:72
  10.0 274.9 %all-reduce.5.cloned.1.call-start = ((), (), s32[]{:S(2)}) async-start(), calls=%async_computation.13 | async-start | bytes 6291456 | tf_op jit(solution)/shard_map/psum | solution.py:158
  11.5 84.3 %copy-start.49 = (f32[384]{0:T(512)}, f32[384]{0:T(512)S(1)}, u32[]{:S(2)}) copy-start(f32[384]{0:T(512)S(1)} %mul.513) | copy-start | bytes 4612
  22.7 30.5 %copy-start.39 = (bf16[1536,6]{0,1:T(8,128)(2,1)}, bf16[1536,6]{0,1:T(8,128)(2,1)S(1)}, u32[]{:S(2)}) copy-start(bf16[1536,6]{0,1:T(8,128)(2,1)S(1)} %reshape.771) | copy-start | bytes 55300
  51.2 39.1 %copy-start.57 = (f32[512]{0:T(512)}, f32[512]{0:T(512)S(1)}, u32[]{:S(2)}) copy-start(f32[512]{0:T(512)S(1)} %add_rsqrt_fusion) | copy-start | bytes 6148
  53.2 5.0 copy-start.42
  55.5 2.4 collective-permute-start.1
  59.5 30.8 %copy-start.2 = (bf16[1,512,1536]{2,1,0:T(8,128)(2,1)S(1)}, bf16[1,512,1536]{2,1,0:T(8,128)(2,1)}, u32[]{:S(2)}) copy-start(bf16[1,512,1536]{2,1,0:T(8,128)(2,1)} %all-gather.9.cloned.1.call-done) | copy-start | bytes 4718596
  94.4 7.8 copy-start.4
  94.6 7.8 copy-start.9
  94.6 9.4 copy-start.6
  95.7 6.0 copy-start.37
  95.8 5.9 copy-start.35
  96.7 13.4 %collective-permute-start = (bf16[1,512,384]{1,2,0:T(8,128)(2,1)}, bf16[1,512,384]{1,2,0:T(8,128)(2,1)}, u32[]{:S(2)}, u32[]{:S(2)}) collective-permute-start(bf16[1,512,384]{1,2,0:T(8,128)(2,1)} %multiply_convert_fusion.9), channel_id=1, source_target_pairs={{0,4},{1,5},{2,6},{3,7},{8,12},{9,13},{10,14},{11,15},{16,20},{17,... | collective-permute-start | bytes 1179656 | tf_op jit(solution)/shard_map/ppermute | solution.py:13
  99.6 12.7 %collective-permute-start.2 = (bf16[1,512,384]{1,2,0:T(8,128)(2,1)}, bf16[1,512,384]{1,2,0:T(8,128)(2,1)}, u32[]{:S(2)}, u32[]{:S(2)}) collective-permute-start(bf16[1,512,384]{1,2,0:T(8,128)(2,1)} %slice_bitcast_fusion.5), channel_id=1, source_target_pairs={{0,4},{1,5},{2,6},{3,7},{8,12},{9,13},{10,14},{11,15},{16,20},{17,... | collective-permute-start | bytes 1179656 | tf_op jit(solution)/shard_map/ppermute | solution.py:13
  155.6 4.0 copy-start.10
  163.7 168.1 %all-gather.17.cloned.1.call-start = ((), (), s32[]{:S(2)}) async-start(), calls=%async_computation.14 | async-start | bytes 7077888 | tf_op jit(solution)/shard_map/all_gather | solution.py:73
  165.9 204.6 %all-gather.21.cloned.1.call-start = ((), (), s32[]{:S(2)}) async-start(), calls=%async_computation.17 | async-start | bytes 1966080 | tf_op jit(solution)/shard_map/all_gather | solution.py:66
  166.7 236.9 %all-gather.19.cloned.1.call-start = ((), (), s32[]{:S(2)}) async-start(), calls=%async_computation.15 | async-start | bytes 3538944 | tf_op jit(solution)/shard_map/all_gather | solution.py:74
  167.4 372.7 %all-reduce.7.cloned.1.call-start = ((), (), s32[]{:S(2)}) async-start(), calls=%async_computation.18 | async-start | bytes 6291456 | tf_op jit(solution)/shard_map/psum | solution.py:186
  287.8 252.4 %copy-start = (f32[512,1536]{1,0:T(8,128)}, f32[512,1536]{1,0:T(8,128)S(1)}, u32[]{:S(2)}) copy-start(f32[512,1536]{1,0:T(8,128)S(1)} %get-tuple-element.267) | copy-start | bytes 9437188
  418.9 332.6 %reduce-scatter.14.cloned.1.call-start = ((), (), s32[]{:S(2)}) async-start(), calls=%async_computation.16 | async-start | bytes 1966080 | tf_op jit(solution)/shard_map/reduce_scatter | solution.py:167
  430.2 323.7 %reduce-scatter.30.cloned.1.call-start = ((), (), s32[]{:S(2)}) async-start(), calls=%async_computation.26 | async-start | bytes 442368
  540.2 3.5 copy-start.54
  540.2 3.5 copy-start.8
  540.2 3.5 copy-start.19
  540.2 3.5 copy-start.44
  540.2 3.5 copy-start.51
  540.2 3.5 copy-start.65
  543.7 3.0 copy-start.12
  543.7 3.0 copy-start.16
  543.7 3.0 copy-start.25
  552.2 3.0 copy-start.1
  568.4 3.0 copy-start.1
  584.6 3.0 copy-start.1
  600.8 3.0 copy-start.1
  617.0 3.0 copy-start.1
  633.2 3.0 copy-start.1
  653.4 51.8 %collective-permute-start.4 = (bf16[1,512,384]{1,2,0:T(8,128)(2,1)}, bf16[1,512,384]{1,2,0:T(8,128)(2,1)}, u32[]{:S(2)}, u32[]{:S(2)}) collective-permute-start(bf16[1,512,384]{1,2,0:T(8,128)(2,1)} %bitcast.100), channel_id=1, source_target_pairs={{4,0},{5,1},{6,2},{7,3},{12,8},{13,9},{14,10},{15,11},{20,16},{21,... | collective-permute-start | bytes 1179656 | tf_op jit(solution)/shard_map/ppermute | solution.py:13
  656.6 44.0 %collective-permute-start.3 = (bf16[1,512,384]{1,2,0:T(8,128)(2,1)}, bf16[1,512,384]{1,2,0:T(8,128)(2,1)}, u32[]{:S(2)}, u32[]{:S(2)}) collective-permute-start(bf16[1,512,384]{1,2,0:T(8,128)(2,1)} %bitcast.90), channel_id=1, source_target_pairs={{4,0},{5,1},{6,2},{7,3},{12,8},{13,9},{14,10},{15,11},{20,16},{21,... | collective-permute-start | bytes 1179656 | tf_op jit(solution)/shard_map/ppermute | solution.py:13
  665.8 5.1 copy-start.24
  665.8 6.0 copy-start.34
  665.8 6.0 copy-start.38
  665.8 6.0 collective-permute-start.5
  700.3 96.4 %reduce-scatter.28.cloned.1.call-start = ((), (), s32[]{:S(2)}) async-start(), calls=%async_computation.25 | async-start | bytes 163840
  705.2 4.7 copy-start.27
  705.2 4.7 copy-start.29
  711.4 4.3 copy-start.66
  715.7 90.0 %reduce-scatter.26.cloned.1.call-start = ((), (), s32[]{:S(2)}) async-start(), calls=%async_computation.24 | async-start | bytes 3538944 | tf_op jit(solution)/shard_map/reduce_scatter | solution.py:300
  722.2 123.4 %reduce-scatter.20.cloned.1.call-start = ((), (), s32[]{:S(2)}) async-start(), calls=%async_computation.21 | async-start | bytes 1327104 | tf_op jit(solution)/shard_map/reduce_scatter | solution.py:291
  725.9 159.9 %reduce-scatter.22.cloned.1.call-start = ((), (), s32[]{:S(2)}) async-start(), calls=%async_computation.22 | async-start | bytes 1327104 | tf_op jit(solution)/shard_map/reduce_scatter | solution.py:294
  728.0 195.8 %reduce-scatter.16.cloned.1.call-start = ((), (), s32[]{:S(2)}) async-start(), calls=%async_computation.19 | async-start | bytes 1966080 | tf_op jit(solution)/shard_map/reduce_scatter | solution.py:269
  728.6 245.7 %reduce-scatter.18.cloned.1.call-start = ((), (), s32[]{:S(2)}) async-start(), calls=%async_computation.20 | async-start | bytes 3981312 | tf_op jit(solution)/shard_map/reduce_scatter | solution.py:285
  734.9 304.4 %reduce-scatter.24.cloned.1.call-start = ((), (), s32[]{:S(2)}) async-start(), calls=%async_computation.23 | async-start | bytes 7077888 | tf_op jit(solution)/shard_map/reduce_scatter | solution.py:297
  738.0 4.0 copy-start.45
  738.0 4.0 copy-start.52
  750.8 2.9 copy-start.68
  750.8 4.6 copy-start.56
  750.9 4.7 copy-start.67
  (35 other events, 59.1 us)
Sparse Core Ops, SparseCore 0:
  9.6 39.7 all-gather.8
  51.3 32.8 all-gather.10
  86.1 24.0 all-gather.12
  112.0 24.0 all-gather.14
  163.8 121.0 all-reduce.4
  287.2 44.5 all-gather.16
  333.4 37.0 all-gather.20
  372.4 31.1 all-gather.18
  419.0 121.0 all-reduce.6
  542.3 34.2 reduce-scatter.13
  700.4 35.1 reduce-scatter.29
  738.2 19.1 reduce-scatter.27
  761.2 44.4 reduce-scatter.25
  808.8 36.7 reduce-scatter.19
  849.0 36.7 reduce-scatter.21
  888.6 35.2 reduce-scatter.15
  927.2 47.0 reduce-scatter.17
  977.5 61.7 reduce-scatter.23
where the time goes:
time: 1060 us; the launch traced here: 1050 us
  waiting for transfers between devices  611 us (58%)
  matrix products  162 us (15%)
  local copies, waits for them, and re-layouts  121 us (11%)
  other arithmetic  75.4 us (7%)
  blocking collectives  51.8 us (5%)
  between operations  16.4 us (2%)
  starting transfers between devices  12.2 us (1%)
    psum x1, waiting for transfers between devices, body(): branch_full = lax.psum(branch_part, 'tp')  116 us
    psum x1, waiting for transfers between devices, body(): d_normed_mid = lax.psum(d_mid_terms, 'tp')  110 us
    reduce_scatter x1, waiting for transfers between devices, body(): lax.psum_scatter(grad_gu.astype(jnp.bfloat16), ('shard', 'ctx'), scatter_...  63 us
    dot_general x24, matrix products, product_t(): lax.dot_general(left, right, (((1,), (1,)), ((), ())), preferred_element_...  58 us
    dot_general x18, matrix products, outer_rows(): lax.dot_general(left, right, (((0,), (0,)), ((), ())), preferred_element_...  52.8 us
    dot_general x18, matrix products, product(): return jnp.dot(left, right, preferred_element_type=jnp.float32)  51.2 us
    reduce_scatter x1, waiting for transfers between devices, body(): lax.psum_scatter(grad_qkv.astype(jnp.bfloat16), ('shard', 'ctx'), scatter...  48.2 us
    all_gather x1, waiting for transfers between devices, body(): lax.all_gather(w_gu, ('shard', 'ctx'), axis=0, tiled=True)  42.5 us
  transfers between devices with their start and end apart: 24, of which 14 were waited for; matrix products, arithmetic and copies ran while one was open for 31% of the time, Pallas kernels for 0%

commit v1 on v0

--- a/solution.py
+++ b/solution.py
@@ -183,7 +183,19 @@
     grad_down = outer_rows(cot_rows, hidden)
     grad_gu = outer_rows(normed_mid, d_both).reshape(model_width, 2, hidden_units)
     d_mid_terms = product_t(d_both, gu_flat)
-    d_normed_mid = lax.psum(d_mid_terms, "tp")
+
+    def put_the_clusters(frame, link_axis="tp"):
+        right_arr = frame
+        num_devices = lax.axis_size(link_axis)
+        for t in [q for q in (1, 2, 4, 8, 16) if q < num_devices]:
+            right_arr = right_arr + lax.ppermute(
+                right_arr,
+                axis_name=link_axis,
+                perm=tuple(((j0, j0 ^ t) for j0 in range(num_devices))),
+            )
+        return right_arr
+
+    d_normed_mid = put_the_clusters(d_mid_terms)
     _, pull_mid = jax.vjp(norm_rows, middle, gain_mlp)
     d_middle_norm, d_gain_mlp_all = pull_mid(d_normed_mid)
     d_middle = d_middle_norm + cot_rows.astype(jnp.float32)

time: 1060 us -> 1130 us (1.066)
  waiting for transfers between devices: 611 us -> 674 us
    ppermute x0 -> x2, waiting for transfers between devices: none -> 216 us  [put_the_clusters(): lax.ppermute(right_arr, axis_name=link_axis, perm=tuple(((j0, j0 ^ t) for...]
    psum x1 -> x0, waiting for transfers between devices: 110 us -> none  [body(): d_normed_mid = lax.psum(d_mid_terms, 'tp')]
    reduce_scatter x1, waiting for transfers between devices: 37.9 us -> 4.5 us  [body(): lax.psum_scatter(grad_ogate.astype(jnp.bfloat16), ('shard', 'ctx'), scatt...]
  transfers between devices with their start and end apart: 24 -> 25, of which waited for: 14 -> 14; matrix products, arithmetic and copies ran while one was open for 31% -> 30% of each run, Pallas kernels for 0% -> 0%
where the time goes in v1:
time: 1130 us; the launch traced here: 1120 us
  waiting for transfers between devices  674 us (60%)
  matrix products  160 us (14%)
  local copies, waits for them, and re-layouts  120 us (11%)
  other arithmetic  82.1 us (7%)
  blocking collectives  51.9 us (5%)
  starting transfers between devices  16.1 us (1%)
  between operations  16 us (1%)
    ppermute x2, waiting for transfers between devices, put_the_clusters(): lax.ppermute(right_arr, axis_name=link_axis, perm=tuple(((j0, j0 ^ t) for...  216 us
    psum x1, waiting for transfers between devices, body(): branch_full = lax.psum(branch_part, 'tp')  116 us
    reduce_scatter x1, waiting for transfers between devices, body(): lax.psum_scatter(grad_gu.astype(jnp.bfloat16), ('shard', 'ctx'), scatter_...  63.4 us
    dot_general x24, matrix products, product_t(): lax.dot_general(left, right, (((1,), (1,)), ((), ())), preferred_element_...  55.1 us
    dot_general x18, matrix products, outer_rows(): lax.dot_general(left, right, (((0,), (0,)), ((), ())), preferred_element_...  53.4 us
    dot_general x18, matrix products, product(): return jnp.dot(left, right, preferred_element_type=jnp.float32)  51.3 us
    reduce_scatter x1, waiting for transfers between devices, body(): lax.psum_scatter(grad_qkv.astype(jnp.bfloat16), ('shard', 'ctx'), scatter...  48.4 us
    all_gather x1, waiting for transfers between devices, body(): lax.all_gather(w_gu, ('shard', 'ctx'), axis=0, tiled=True)  42.9 us
  transfers between devices with their start and end apart: 25, of which 14 were waited for; matrix products, arithmetic and copies ran while one was open for 30% of the time, Pallas kernels for 0%

profile of v1, /device:TPU:0, one launch (start us, length us, event | category | flops | bytes accessed | tf_op | source)
XLA Modules:
  0.0 1119.6 jit_solution(7039860153011921604)
XLA Ops:
  12.0 10.6 all-gather
  24.8 24.6 %all-gather.9.cloned.1.call-done = bf16[1,512,1536]{2,1,0:T(8,128)(2,1)} async-done(((bf16[1,128,1536]{2,1,0:T(8,128)(2,1)}), bf16[1,512,1536]{2,1,0:T(8,128)(2,1)}) %all-gather.9.cloned.1.call-update) | async-done | bytes 1572880 | tf_op jit(solution)/shard_map/all_gather | solution.py:65
  59.5 24.7 %all-gather.11.cloned.1.call-done = bf16[1536,3,384]{2,0,1:T(8,128)(2,1)} async-done(((bf16[192,3,384]{2,0,1:T(8,128)(2,1)}), bf16[1536,3,384]{2,0,1:T(8,128)(2,1)}) %all-gather.11.cloned.1.call-update) | async-done | bytes 3538960 | tf_op jit(solution)/shard_map/all_gather | solution.py:69
  84.2 6.1 copy.92
  90.3 4.1 fusion.41
  96.8 2.9 collective-permute-start
  99.7 2.1 collective-permute-start.2
  106.9 3.3 fusion.74
  110.2 2.2 copy.94
  112.3 2.2 copy.101
  118.7 37.0 %while.31 = (s32[]{:T(128)}, f32[6,512,64]{1,2,0:T(8,128)}, f32[6,512]{1,0:T(8,128)S(1)}, bf16[6,512,64]{2,1,0:T(8,128)(2,1)}, bf16[6,1024,64]{2,1,0:T(8,128)(2,...) while((s32[]{:T(128)}, f32[6,512,64]{1,2,0:T(8,128)}, ...), condition=%wide.region_8.9_spmd, body=%wide.region_5.8_spmd.sunk | while | flops 139460096 | bytes 7643265 | solution.py:151
  122.6 2.2 fusion.162
  128.7 2.3 fusion.162
  134.9 2.2 fusion.162
  141.1 2.2 fusion.162
  147.2 2.2 fusion.162
  153.4 2.2 fusion.162
  156.3 3.5 fusion.84
  159.8 4.0 fusion.126
  168.9 116.1 %all-reduce.4.cloned.1.call-done = f32[512,1536]{1,0:T(8,128)} async-done(((f32[512,1536]{1,0:T(8,128)}), f32[512,1536]{1,0:T(8,128)}) %all-reduce.4.cloned.1.call-update) | async-done | bytes 3145744 | tf_op jit(solution)/shard_map/psum | solution.py:158
  285.0 2.8 multiply_reduce_fusion.5
  289.0 42.9 %all-gather.17.cloned.1.call-done = bf16[1536,2,1024]{2,0,1:T(8,128)(2,1)} async-done(((bf16[192,2,1024]{2,0,1:T(8,128)(2,1)}), bf16[1536,2,1024]{2,0,1:T(8,128)(2,1)}) %all-gather.17.cloned.1.call-update) | async-done | bytes 6291472 | tf_op jit(solution)/shard_map/all_gather | solution.py:73
  331.9 8.7 copy.104
  340.6 8.1 fusion.36
  348.6 22.0 %all-gather.21.cloned.1.call-done = bf16[1,512,1536]{2,1,0:T(8,128)(2,1)} async-done(((bf16[1,128,1536]{2,1,0:T(8,128)(2,1)}), bf16[1,512,1536]{2,1,0:T(8,128)(2,1)}) %all-gather.21.cloned.1.call-update) | async-done | bytes 1572880 | tf_op jit(solution)/shard_map/all_gather | solution.py:66
  370.6 33.1 %all-gather.19.cloned.1.call-done = bf16[1536,1024]{1,0:T(8,128)(2,1)} async-done(((bf16[192,1024]{1,0:T(8,128)(2,1)}), bf16[1536,1024]{1,0:T(8,128)(2,1)}) %all-gather.19.cloned.1.call-update) | async-done | bytes 3145744 | tf_op jit(solution)/shard_map/all_gather | solution.py:74
  403.7 6.0 fusion.52
  409.7 8.8 convolution_bitcast_fusion.2
  420.0 3.0 fusion.47
  423.1 91.3 %collective-permute-done.3 = f32[512,1536]{1,0:T(8,128)} collective-permute-done((f32[512,1536]{1,0:T(8,128)}, f32[512,1536]{1,0:T(8,128)}, u32[]{:S(2)}, u32[]{:S(2)}) %collective-permute-start.3) | collective-permute-done | bytes 3145760 | tf_op jit(solution)/shard_map/ppermute | solution.py:191
  514.4 5.1 add.262
  519.5 2.4 collective-permute-start.4
  526.5 6.4 convolution_convert_fusion.2
  533.2 124.4 %collective-permute-done.4 = f32[512,1536]{1,0:T(8,128)} collective-permute-done((f32[512,1536]{1,0:T(8,128)}, f32[512,1536]{1,0:T(8,128)}, u32[]{:S(2)}, u32[]{:S(2)}) %collective-permute-start.4) | collective-permute-done | bytes 3145760 | tf_op jit(solution)/shard_map/ppermute | solution.py:191
  657.6 4.4 multiply_reduce_fusion.1
  662.1 4.0 fusion.46
  668.0 2.2 copy.105
  671.7 97.3 %while.32 = (s32[]{:T(128)}, f32[6,512,64]{1,2,0:T(8,128)}, f32[6,1024,64]{1,2,0:T(8,128)}, f32[6,1024,64]{1,2,0:T(8,128)}, f32[6,512]{1,0:T(8,128)}, /*index=5*...) while((s32[]{:T(128)}, f32[6,512,64]{1,2,0:T(8,128)}, ...), condition=%wide.region_17.18_spmd, body=%wide.region_13.17_spmd.sunk | while | flops 342981632 | bytes 20376776 | solution.py:228
  691.0 2.1 multiply_reduce_fusion.11
  739.6 2.1 multiply_reduce_fusion.11
  755.9 2.1 multiply_reduce_fusion.11
  771.0 2.1 slice.88
  786.9 2.3 fusion.80
  792.1 2.7 rev.7
  796.1 4.1 reduce-window.16
  810.9 2.7 rev.8
  815.6 2.6 convolution_convert_fusion.6
  820.3 2.3 multiply_reduce_fusion.6
  827.3 2.3 convolution_bitcast_fusion.3
  831.0 3.4 multiply_reduce_fusion.2
  835.3 3.7 convolution_convert_fusion.5
  839.1 4.0 convolution_convert_fusion.4
  843.2 3.1 maximum_convert_fusion
  846.2 4.0 copy.114
  850.2 7.5 convolution_convert_fusion
  858.7 5.8 convolution_convert_fusion.1
  870.4 41.2 %all-reduce.1 = (f32[24]{0:T(128)}, f32[1536]{0:T(1024)}, f32[1536]{0:T(1024)}, f32[2,64]{1,0:T(2,128)}) all-reduce(f32[24]{0:T(128)S(1)} %dynamic_update_slice.28, f32[1536]{0:T(1024)S(1)} %get-tuple-element.207, f32[1536]{0:T(1024)S(1)} %fusion.108, ...), channel_id=1, replica_groups=mesh['shard'=4,'ctx'=2,'tp'=4] {'shard','ctx','tp'}, use_global_device_ids=true, to_apply=%region_29.30 | all-reduce | flops 3224 | bytes 25792 | tf_op jit(solution)/shard_map/psum | solution.py:320
  912.4 4.5 reduce-scatter.20.cloned.1.call-done
  918.6 38.6 %reduce-scatter.22.cloned.1.call-done = bf16[192,384]{1,0:T(8,128)(2,1)} async-done(((bf16[1536,384]{1,0:T(8,128)(2,1)}), bf16[192,384]{1,0:T(8,128)(2,1)}) %reduce-scatter.22.cloned.1.call-update) | async-done | bytes 147472 | tf_op jit(solution)/shard_map/reduce_scatter | solution.py:306
  958.8 63.4 %reduce-scatter.24.cloned.1.call-done = bf16[192,2,1024]{2,0,1:T(8,128)(2,1)} async-done(((bf16[1536,2,1024]{2,0,1:T(8,128)(2,1)}), bf16[192,2,1024]{2,0,1:T(8,128)(2,1)}) %reduce-scatter.24.cloned.1.call-update) | async-done | bytes 786448 | tf_op jit(solution)/shard_map/reduce_scatter | solution.py:309
  1022.2 3.1 copy.116
  1025.3 34.5 %reduce-scatter.16.cloned.1.call-done = bf16[1,128,1536]{2,1,0:T(8,128)(2,1)} async-done(((bf16[1,512,1536]{2,1,0:T(8,128)(2,1)}), bf16[1,128,1536]{2,1,0:T(8,128)(2,1)}) %reduce-scatter.16.cloned.1.call-update) | async-done | bytes 393232 | tf_op jit(solution)/shard_map/reduce_scatter | solution.py:281
  1059.8 2.5 fusion.83
  1062.2 48.4 %reduce-scatter.18.cloned.1.call-done = bf16[192,3,384]{2,0,1:T(8,128)(2,1)} async-done(((bf16[1536,3,384]{2,0,1:T(8,128)(2,1)}), bf16[192,3,384]{2,0,1:T(8,128)(2,1)}) %reduce-scatter.18.cloned.1.call-update) | async-done | bytes 442384 | tf_op jit(solution)/shard_map/reduce_scatter | solution.py:297
  (405 shorter events, 213.3 us)
Async XLA Ops:
  7.2 17.5 %copy-start.68 = (f32[24]{0:T(128)S(1)}, f32[24]{0:T(128)}, u32[]{:S(2)}) copy-start(f32[24]{0:T(128)} %param.24) | copy-start | bytes 292
  7.2 42.2 %all-gather.9.cloned.1.call-start = ((), (), s32[]{:S(2)}) async-start(), calls=%async_computation.9 | async-start | bytes 1966080 | tf_op jit(solution)/shard_map/all_gather | solution.py:65
  7.9 76.3 %all-gather.11.cloned.1.call-start = ((), (), s32[]{:S(2)}) async-start(), calls=%async_computation.10 | async-start | bytes 3981312 | tf_op jit(solution)/shard_map/all_gather | solution.py:69
  8.7 42.5 %copy-start.58 = (f32[1536]{0:T(1024)S(1)}, f32[1536]{0:T(1024)}, u32[]{:S(2)}) copy-start(f32[1536]{0:T(1024)} %param.29) | copy-start | bytes 18436
  8.7 147.1 %all-gather.13.cloned.1.call-start = ((), (), s32[]{:S(2)}) async-start(), calls=%async_computation.11 | async-start | bytes 1327104 | tf_op jit(solution)/shard_map/all_gather | solution.py:71
  9.4 150.3 %all-gather.15.cloned.1.call-start = ((), (), s32[]{:S(2)}) async-start(), calls=%async_computation.12 | async-start | bytes 1327104 | tf_op jit(solution)/shard_map/all_gather | solution.py:72
  10.0 275.0 %all-reduce.4.cloned.1.call-start = ((), (), s32[]{:S(2)}) async-start(), calls=%async_computation.13 | async-start | bytes 6291456 | tf_op jit(solution)/shard_map/psum | solution.py:158
  11.6 84.3 %copy-start.48 = (f32[384]{0:T(512)}, f32[384]{0:T(512)S(1)}, u32[]{:S(2)}) copy-start(f32[384]{0:T(512)S(1)} %mul.513) | copy-start | bytes 4612
  22.8 30.4 %copy-start.38 = (bf16[1536,6]{0,1:T(8,128)(2,1)}, bf16[1536,6]{0,1:T(8,128)(2,1)S(1)}, u32[]{:S(2)}) copy-start(bf16[1536,6]{0,1:T(8,128)(2,1)S(1)} %reshape.771) | copy-start | bytes 55300
  51.2 39.1 %copy-start.56 = (f32[512]{0:T(512)}, f32[512]{0:T(512)S(1)}, u32[]{:S(2)}) copy-start(f32[512]{0:T(512)S(1)} %add_rsqrt_fusion) | copy-start | bytes 6148
  53.2 5.0 copy-start.41
  55.5 2.4 collective-permute-start.1
  59.5 30.9 %copy-start.2 = (bf16[1,512,1536]{2,1,0:T(8,128)(2,1)S(1)}, bf16[1,512,1536]{2,1,0:T(8,128)(2,1)}, u32[]{:S(2)}) copy-start(bf16[1,512,1536]{2,1,0:T(8,128)(2,1)} %all-gather.9.cloned.1.call-done) | copy-start | bytes 4718596
  94.5 7.9 copy-start.4
  94.6 7.8 copy-start.8
  94.6 9.4 copy-start.6
  95.7 6.0 copy-start.36
  95.9 5.9 copy-start.34
  96.8 13.4 %collective-permute-start = (bf16[1,512,384]{1,2,0:T(8,128)(2,1)}, bf16[1,512,384]{1,2,0:T(8,128)(2,1)}, u32[]{:S(2)}, u32[]{:S(2)}) collective-permute-start(bf16[1,512,384]{1,2,0:T(8,128)(2,1)} %multiply_convert_fusion.9), channel_id=1, source_target_pairs={{0,4},{1,5},{2,6},{3,7},{8,12},{9,13},{10,14},{11,15},{16,20},{17,... | collective-permute-start | bytes 1179656 | tf_op jit(solution)/shard_map/ppermute | solution.py:13
  99.7 12.7 %collective-permute-start.2 = (bf16[1,512,384]{1,2,0:T(8,128)(2,1)}, bf16[1,512,384]{1,2,0:T(8,128)(2,1)}, u32[]{:S(2)}, u32[]{:S(2)}) collective-permute-start(bf16[1,512,384]{1,2,0:T(8,128)(2,1)} %slice_bitcast_fusion.5), channel_id=1, source_target_pairs={{0,4},{1,5},{2,6},{3,7},{8,12},{9,13},{10,14},{11,15},{16,20},{17,... | collective-permute-start | bytes 1179656 | tf_op jit(solution)/shard_map/ppermute | solution.py:13
  155.7 4.1 copy-start.9
  163.8 168.1 %all-gather.17.cloned.1.call-start = ((), (), s32[]{:S(2)}) async-start(), calls=%async_computation.14 | async-start | bytes 7077888 | tf_op jit(solution)/shard_map/all_gather | solution.py:73
  166.0 204.6 %all-gather.21.cloned.1.call-start = ((), (), s32[]{:S(2)}) async-start(), calls=%async_computation.17 | async-start | bytes 1966080 | tf_op jit(solution)/shard_map/all_gather | solution.py:66
  166.8 236.9 %all-gather.19.cloned.1.call-start = ((), (), s32[]{:S(2)}) async-start(), calls=%async_computation.15 | async-start | bytes 3538944 | tf_op jit(solution)/shard_map/all_gather | solution.py:74
  167.5 697.2 %reduce-scatter.14.cloned.1.call-start = ((), (), s32[]{:S(2)}) async-start(), calls=%async_computation.16 | async-start | bytes 1966080 | tf_op jit(solution)/shard_map/reduce_scatter | solution.py:167
  409.6 8.9 copy-start.21
  409.6 8.9 copy-start.22
  409.7 10.3 copy-start.67
  409.7 10.3 copy-start.69
  418.5 95.9 %collective-permute-start.3 = (f32[512,1536]{1,0:T(8,128)}, f32[512,1536]{1,0:T(8,128)}, u32[]{:S(2)}, u32[]{:S(2)}) collective-permute-start(f32[512,1536]{1,0:T(8,128)} %convolution_bitcast_fusion.2), channel_id=1, source_target_pairs={{0,1},{1,0},{2,3},{3,2},{4,5},{5,4},{6,7},{7,6},{8,9},{9,8},{10,11... | collective-permute-start | bytes 9437192 | tf_op jit(solution)/shard_map/ppermute | solution.py:191
  423.0 443.5 %reduce-scatter.26.cloned.1.call-start = ((), (), s32[]{:S(2)}) async-start(), calls=%async_computation.23 | async-start | bytes 3538944 | tf_op jit(solution)/shard_map/reduce_scatter | solution.py:312
  519.5 138.1 %collective-permute-start.4 = (f32[512,1536]{1,0:T(8,128)}, f32[512,1536]{1,0:T(8,128)}, u32[]{:S(2)}, u32[]{:S(2)}) collective-permute-start(f32[512,1536]{1,0:T(8,128)} %add.262), channel_id=1, source_target_pairs={{0,2},{1,3},{2,0},{3,1},{4,6},{5,7},{6,4},{7,5},{8,10},{9,11},{10,... | collective-permute-start | bytes 9437192 | tf_op jit(solution)/shard_map/ppermute | solution.py:191
  532.9 335.9 %reduce-scatter.30.cloned.1.call-start = ((), (), s32[]{:S(2)}) async-start(), calls=%async_computation.25 | async-start | bytes 442368
  533.1 128.9 %copy-start.51 = (f32[512]{0:T(512)S(1)}, f32[512]{0:T(512)}, u32[]{:S(2)}) copy-start(f32[512]{0:T(512)} %copy-done.50) | copy-start | bytes 6148
  533.1 128.9 %copy-start.18 = (bf16[1,512,1536]{2,1,0:T(8,128)(2,1)S(1)}, bf16[1,512,1536]{2,1,0:T(8,128)(2,1)}, u32[]{:S(2)}) copy-start(bf16[1,512,1536]{2,1,0:T(8,128)(2,1)} %all-gather.21.cloned.1.call-done) | copy-start | bytes 4718596
  533.2 128.9 %copy-start.43 = (f32[1536]{0:T(1024)S(1)}, f32[1536]{0:T(1024)}, u32[]{:S(2)}) copy-start(f32[1536]{0:T(1024)} %param.30) | copy-start | bytes 18436
  533.2 128.9 %copy-start.52 = (f32[512]{0:T(512)S(1)}, f32[512]{0:T(512)}, u32[]{:S(2)}) copy-start(f32[512]{0:T(512)} %fusion.113) | copy-start | bytes 6148
  533.2 128.9 %copy-start.64 = (bf16[512]{0:T(512)(128)(2,1)S(1)}, bf16[512]{0:T(512)(128)(2,1)}, u32[]{:S(2)}) copy-start(bf16[512]{0:T(512)(128)(2,1)} %convert_convert_fusion) | copy-start | bytes 3076
  662.1 4.0 copy-start.11
  662.1 4.0 copy-start.15
  662.1 4.0 copy-start.24
  671.7 3.0 copy-start.1
  736.6 3.0 copy-start.1
  752.8 3.0 copy-start.1
  773.1 51.8 %collective-permute-start.6 = (bf16[1,512,384]{1,2,0:T(8,128)(2,1)}, bf16[1,512,384]{1,2,0:T(8,128)(2,1)}, u32[]{:S(2)}, u32[]{:S(2)}) collective-permute-start(bf16[1,512,384]{1,2,0:T(8,128)(2,1)} %bitcast.100), channel_id=1, source_target_pairs={{4,0},{5,1},{6,2},{7,3},{12,8},{13,9},{14,10},{15,11},{20,16},{21,... | collective-permute-start | bytes 1179656 | tf_op jit(solution)/shard_map/ppermute | solution.py:13
  776.3 44.0 %collective-permute-start.5 = (bf16[1,512,384]{1,2,0:T(8,128)(2,1)}, bf16[1,512,384]{1,2,0:T(8,128)(2,1)}, u32[]{:S(2)}, u32[]{:S(2)}) collective-permute-start(bf16[1,512,384]{1,2,0:T(8,128)(2,1)} %bitcast.90), channel_id=1, source_target_pairs={{4,0},{5,1},{6,2},{7,3},{12,8},{13,9},{14,10},{15,11},{20,16},{21,... | collective-permute-start | bytes 1179656 | tf_op jit(solution)/shard_map/ppermute | solution.py:13
  785.4 5.1 copy-start.23
  785.4 6.1 copy-start.33
  785.4 6.1 copy-start.37
  785.4 6.0 collective-permute-start.7
  819.9 91.7 %reduce-scatter.28.cloned.1.call-start = ((), (), s32[]{:S(2)}) async-start(), calls=%async_computation.24 | async-start | bytes 163840
  824.9 4.7 copy-start.26
  824.9 4.7 copy-start.28
  835.3 81.7 %reduce-scatter.20.cloned.1.call-start = ((), (), s32[]{:S(2)}) async-start(), calls=%async_computation.20 | async-start | bytes 1327104 | tf_op jit(solution)/shard_map/reduce_scatter | solution.py:303
  839.0 118.1 %reduce-scatter.22.cloned.1.call-start = ((), (), s32[]{:S(2)}) async-start(), calls=%async_computation.21 | async-start | bytes 1327104 | tf_op jit(solution)/shard_map/reduce_scatter | solution.py:306
  843.1 179.1 %reduce-scatter.24.cloned.1.call-start = ((), (), s32[]{:S(2)}) async-start(), calls=%async_computation.22 | async-start | bytes 7077888 | tf_op jit(solution)/shard_map/reduce_scatter | solution.py:309
  846.2 4.0 copy-start.44
  846.2 4.0 copy-start.53
  857.7 202.1 %reduce-scatter.16.cloned.1.call-start = ((), (), s32[]{:S(2)}) async-start(), calls=%async_computation.18 | async-start | bytes 1966080 | tf_op jit(solution)/shard_map/reduce_scatter | solution.py:281
  858.3 252.3 %reduce-scatter.18.cloned.1.call-start = ((), (), s32[]{:S(2)}) async-start(), calls=%async_computation.19 | async-start | bytes 3981312 | tf_op jit(solution)/shard_map/reduce_scatter | solution.py:297
  864.5 4.0 copy-start.45
  864.5 4.0 copy-start.66
  864.5 5.7 copy-start.55
  864.5 5.8 copy-start.65
  (36 other events, 67.0 us)
Sparse Core Ops, SparseCore 0:
  9.6 39.7 all-gather.8
  51.3 32.8 all-gather.10
  86.1 24.0 all-gather.12
  111.9 24.1 all-gather.14
  163.9 121.0 all-reduce.3
  287.3 44.5 all-gather.16
  333.5 37.0 all-gather.20
  372.5 31.1 all-gather.18
  423.2 58.4 reduce-scatter.13
  533.0 44.3 reduce-scatter.25
  820.1 36.0 reduce-scatter.29
  858.9 19.1 reduce-scatter.27
  881.9 34.9 reduce-scatter.19
  920.4 36.7 reduce-scatter.21
  960.4 61.7 reduce-scatter.23
  1024.4 35.2 reduce-scatter.15
  1063.5 47.0 reduce-scatter.17
